TPU v7x, 512 devices: a whole 4x8x8 slice. The times are simulated.
512 devices in a mesh: rep: 4 (over x), exp: 128 (over z, y, core).
Axes of the slice: x: 4, y: 8, z: 8, core: 2. Of those that a mesh axis runs over, the one named last changes fastest.
Arguments:
- tokens: bfloat16 [16384, 2048], P('exp', 'rep'), may hold values from -6 to 6
- expert_ids: int32 [16384, 8], P('exp'), may hold values from 0 to 127, all different within a row; in each aligned block of 128 rows (0 to 127, 128 to 255, ...) at most 12 rows name the same one
- route_weights: float32 [16384, 8], P('exp'), may hold values from 0.05 to 1
- w_gate: bfloat16 [128, 768, 2048], P('exp', None, 'rep'), may hold values from -0.125 to 0.125
- w_up: bfloat16 [128, 768, 2048], P('exp', None, 'rep'), may hold values from -0.125 to 0.125
- w_down: bfloat16 [128, 768, 2048], P('exp', None, 'rep'), may hold values from -0.21875 to 0.21875
Outputs:
- mixed: bfloat16 [16384, 2048], P('exp', 'rep')
Inputs may be any that keep to these rules, and one draw needn't show every extreme that they name: `expert_ids`: each token names 8 different experts. Within the rows of one index of exp (aligned blocks of 128 tokens) no expert is named more than 12 times, a bound that some block reaches.
All inputs are finite; a program needn't handle non-finite values.
Results may differ from a plain program's by a relative error of at most 0.0058.
Values may be sent and summed in bfloat16 or wider, within the bound.
A program may use at most 64 MiB of HBM per device.

v0:
```python
import jax
import jax.numpy as jnp
from jax import lax
from jax.sharding import PartitionSpec as P

EXPERTS = 128


def local(tokens, expert_ids, route_weights, w_gate, w_up, w_down):
    tok_rows = expert_ids.shape[0]
    top_count = expert_ids.shape[1]
    local_experts = w_gate.shape[0]
    replicas = lax.axis_size("rep")
    replica_index = lax.axis_index("rep")
    full_cap = replicas * max(1, tok_rows * top_count * 3 // (8 * EXPERTS))
    slot_cap = full_cap // replicas
    assigned = expert_ids.reshape(-1)
    onehot = (assigned[:, None] == jnp.arange(EXPERTS, dtype=jnp.int32)[None, :]).astype(jnp.int32)
    before = jnp.cumsum(onehot, axis=0) - onehot
    slot_ids = jnp.sum(before * onehot, axis=1)
    owned = slot_ids % replicas == replica_index
    target = assigned * slot_cap + slot_ids // replicas
    destination = jnp.where(owned, target, EXPERTS * slot_cap)
    probs = route_weights / jnp.sum(route_weights, axis=1, keepdims=True)
    full_rows = lax.all_gather(tokens, "rep", axis=1, tiled=True)
    width = full_rows.shape[1]
    repeated = jnp.repeat(full_rows, top_count, axis=0)
    outgoing = (
        jnp.zeros((EXPERTS * slot_cap, width), jnp.bfloat16)
        .at[destination]
        .set(repeated, mode="drop")
    )
    outgoing = outgoing.reshape(EXPERTS, slot_cap, width)
    arrived = lax.all_to_all(outgoing, "exp", split_axis=0, concat_axis=1, tiled=True)
    gate_sum = jnp.einsum(
        "esd,efd->esf",
        arrived,
        lax.all_gather(w_gate, "rep", axis=2, tiled=True),
        preferred_element_type=jnp.float32,
    )
    up_sum = jnp.einsum(
        "esd,efd->esf",
        arrived,
        lax.all_gather(w_up, "rep", axis=2, tiled=True),
        preferred_element_type=jnp.float32,
    )
    hidden = (jax.nn.silu(gate_sum) * up_sum).astype(jnp.bfloat16)
    expert_out = jnp.einsum(
        "esf,efd->esd",
        hidden,
        lax.all_gather(w_down, "rep", axis=2, tiled=True),
        preferred_element_type=jnp.float32,
    ).astype(jnp.bfloat16)
    owners = expert_out.shape[1] // slot_cap
    share = width // replicas
    split_out = expert_out.reshape(local_experts, owners, slot_cap, replicas, share)
    homed = lax.all_to_all(
        lax.all_to_all(split_out, "rep", split_axis=3, concat_axis=3, tiled=True),
        "exp",
        split_axis=1,
        concat_axis=1,
        tiled=True,
    )
    ordered = jnp.swapaxes(homed, 0, 1).reshape(EXPERTS * full_cap, share)
    picked = ordered[assigned * full_cap + slot_ids].astype(jnp.float32)
    weighted = picked.reshape(tok_rows, top_count, share) * probs[:, :, None]
    return jnp.sum(weighted, axis=1).astype(jnp.bfloat16)


def solution(mesh):
    return jax.shard_map(
        local,
        mesh=mesh,
        in_specs=(
            P("exp", "rep"),
            P("exp", None),
            P("exp", None),
            P("exp", None, "rep"),
            P("exp", None, "rep"),
            P("exp", None, "rep"),
        ),
        out_specs=P("exp", "rep"),
        check_vma=False,
    )
```

profile of v0, /device:TPU:8, one launch (start us, length us, event | category | flops | bytes accessed | tf_op | source)
XLA Modules:
  0.0 256.1 jit_solution(238828360793560490)
XLA Ops:
  6.5 0.7 all-gather.4.cloned.1.call-update
  7.3 0.7 all-gather.6.cloned.1.call-update
  8.1 0.7 all-gather.8.cloned.1.call-update
  8.8 0.1 copy.24
  9.1 0.2 fusion.25
  9.5 0.1 copy.27
  10.0 0.4 fusion.24
  10.4 13.1 %all_gather.12 = bf16[128,2048]{1,0:T(8,128)(2,1)S(1)} all-gather(bf16[128,512]{1,0:T(8,128)(2,1)S(1)} %copy-done), channel_id=1, replica_groups=mesh['rep'=4,'exp'=128] {'rep'}, dimensions={1}, use_global_device_ids=true | all-gather | bytes 655360 | tf_op jit(solution)/shard_map/all_gather | solution.py:25
  23.5 7.7 %scatter_custom_fusion = bf16[384,2048]{1,0:T(8,128)(2,1)} fusion(s32[1024]{0:T(1024)S(1)} %bitcast.42, bf16[128,2048]{1,0:T(8,128)(2,1)S(1)} %all_gather.12, bf16[]{:T(256)} %constant.41.clone.1), kind=kCustom, calls=%fused_computation.2 | custom fusion | bytes 2097154 | tf_op jit(solution)/shard_map/scatter | solution.py:31
  31.2 4.0 %reshape.193 = bf16[128,3,2048]{2,1,0:T(4,128)(2,1)S(1)} reshape(bf16[384,2048]{1,0:T(8,128)(2,1)} %scatter_custom_fusion) | data formatting | bytes 3145728 | tf_op jit(solution)/shard_map/reshape | solution.py:33
  35.2 71.3 %all_to_all.19 = bf16[128,3,2048]{2,1,0:T(4,128)(2,1)} all-to-all(bf16[128,3,2048]{2,1,0:T(4,128)(2,1)S(1)} %reshape.193), channel_id=1, replica_groups=mesh['rep'=4,'exp'=128] {'exp'}, dimensions={0} | all-to-all | bytes 3145728 | tf_op jit(solution)/shard_map/all_to_all | solution.py:34
  106.5 3.9 %reshape.194 = bf16[384,2048]{1,0:T(8,128)(2,1)S(1)} reshape(bf16[128,3,2048]{2,1,0:T(4,128)(2,1)} %all_to_all.19) | data formatting | bytes 3145728 | tf_op jit(solution)/shard_map/reshape.10
  110.5 4.4 %fusion.6 = f32[384,768]{1,0:T(8,128)} fusion(bf16[384,2048]{1,0:T(8,128)(2,1)S(1)} %reshape.194, bf16[1,768,2048]{2,1,0:T(8,128)(2,1)} %all-gather.4.cloned.1.call-done), kind=kOutput, calls=%fused_computation.8 | convolution fusion | flops 1207959552 | bytes 5898240 | tf_op jit(solution)/shard_map/esd,efd->esf/dot_general | solution.py:35
  114.9 38.3 %all-gather.8.cloned.1.call-done = bf16[1,768,2048]{2,1,0:T(8,128)(2,1)} async-done(((bf16[1,768,512]{2,1,0:T(8,128)(2,1)}), bf16[1,768,2048]{2,1,0:T(8,128)(2,1)}) %all-gather.8.cloned.1.call-update) | async-done | bytes 3145744 | tf_op jit(solution)/shard_map/all_gather | solution.py:51
  153.2 6.3 %fusion.8 = bf16[384,2048]{1,0:T(8,128)(2,1)S(1)} fusion(bf16[1,768,2048]{2,1,0:T(8,128)(2,1)} %all-gather.8.cloned.1.call-done, bf16[384,2048]{1,0:T(8,128)(2,1)S(1)} %reshape.194, bf16[1,768,2048]{2,1,0:T(8,128)(2,1)} %all-gather.6.cloned.1.call-done, f32[384,768]{1,0:T(8,128)} %fusion.6), kind=kOutput, calls=%fused_computation.10 | convolution fusion | flops 2418475008 | bytes 10616832 | tf_op jit(solution)/shard_map/esf,efd->esd/dot_general | solution.py:48
  159.5 1.2 reshape.198
  160.7 0.3 copy.29
  161.1 23.5 %all_to_all.20 = bf16[1,128,3,4,512]{4,1,2,0,3:T(8,128)(2,1)S(1)} all-to-all(bf16[1,128,3,4,512]{4,1,2,0,3:T(8,128)(2,1)S(1)} %copy.29), channel_id=1, replica_groups=mesh['rep'=4,'exp'=128] {'rep'}, dimensions={3} | all-to-all | bytes 3145728 | tf_op jit(solution)/shard_map/all_to_all | solution.py:58
  184.6 2.4 copy.30
  187.0 14.3 %all-to-all-start.2 = ((bf16[1,128,3,4,512]{4,3,2,0,1:T(4,128)(2,1)}), bf16[1,128,3,4,512]{4,3,2,0,1:T(4,128)(2,1)S(1)}, u32[]{:S(2)}, u32[]{:S(2)}) async-start(bf16[1,128,3,4,512]{4,3,2,0,1:T(4,128)(2,1)} %copy.30), calls=%async_computation.2 | async-start | bytes 3145728 | tf_op jit(solution)/shard_map/all_to_all | solution.py:57
  201.4 42.4 %all-to-all-done.2 = bf16[1,128,3,4,512]{4,3,2,0,1:T(4,128)(2,1)S(1)} async-done(((bf16[1,128,3,4,512]{4,3,2,0,1:T(4,128)(2,1)}), bf16[1,128,3,4,512]{4,3,2,0,1:T(4,128)(2,1)S(1)}, u32[]{:S(2)}, u32[]{:S(2)}) %all-to-all-start.2) | async-done | bytes 1572896 | tf_op jit(solution)/shard_map/all_to_all | solution.py:57
  243.8 0.4 reshape_transpose.3
  244.2 4.0 %gather_fusion = bf16[1024,512]{1,0:T(8,128)(2,1)S(1)} fusion(bf16[1536,512]{1,0:T(8,128)(2,1)S(1)} %reshape_transpose.3, s32[1024]{0:T(1024)S(1)} %broadcast_clamp_fusion), kind=kCustom, calls=%fused_computation | custom fusion | bytes 2101248 | tf_op jit(solution)/shard_map/gather | solution.py:65
  248.2 1.3 fusion.11
  (28 shorter events, 1.1 us)
Async XLA Ops:
  6.5 2.2 copy-start.1
  6.5 103.9 %all-gather.4.cloned.1.call-start = ((), (), s32[]{:S(2)}) async-start(), calls=%async_computation.3 | async-start | bytes 3932160 | tf_op jit(solution)/shard_map/all_gather | solution.py:38
  7.3 107.6 %all-gather.6.cloned.1.call-start = ((), (), s32[]{:S(2)}) async-start(), calls=%async_computation.4 | async-start | bytes 3932160 | tf_op jit(solution)/shard_map/all_gather | solution.py:44
  8.0 145.2 %all-gather.8.cloned.1.call-start = ((), (), s32[]{:S(2)}) async-start(), calls=%async_computation.5 | async-start | bytes 3932160 | tf_op jit(solution)/shard_map/all_gather | solution.py:51
  9.4 1.0 copy-start
  186.9 14.3 %copy-start.2 = (f32[128,8]{0,1:T(8,128)S(1)}, f32[128,8]{0,1:T(8,128)}, u32[]{:S(2)}) copy-start(f32[128,8]{0,1:T(8,128)} %param.8) | copy-start | bytes 12292
  187.0 56.9 %all-to-all-start.2 = ((bf16[1,128,3,4,512]{4,3,2,0,1:T(4,128)(2,1)}), bf16[1,128,3,4,512]{4,3,2,0,1:T(4,128)(2,1)S(1)}, u32[]{:S(2)}, u32[]{:S(2)}) async-start(bf16[1,128,3,4,512]{4,3,2,0,1:T(4,128)(2,1)} %copy.30), calls=%async_computation.2 | async-start | bytes 3145728 | tf_op jit(solution)/shard_map/all_to_all | solution.py:57
Sparse Core Ops, SparseCore 0:
  9.4 49.3 all-gather.3
  60.9 45.0 all-gather.5
  108.1 45.0 all-gather.7
where the time goes:
time: 257 us; the launch traced here: 256 us
  blocking collectives  108 us (42%)
  waiting for transfers between devices  82.9 us (32%)
  local copies, waits for them, and re-layouts  24.8 us (10%)
  starting transfers between devices  14.4 us (6%)
  between operations  13.3 us (5%)
  matrix products  10.7 us (4%)
    all_to_all x1, blocking collectives, local(): lax.all_to_all(outgoing, 'exp', split_axis=0, concat_axis=1, tiled=True)  71.3 us
    all_to_all x1, waiting for transfers between devices, local(): lax.all_to_all(lax.all_to_all(split_out, 'rep', split_axis=3, concat_axis...  42.4 us
    all_gather x1, waiting for transfers between devices, local(): lax.all_gather(w_down, 'rep', axis=2, tiled=True)  38.3 us
    all_to_all x1, blocking collectives, local(): lax.all_to_all(split_out, 'rep', split_axis=3, concat_axis=3, tiled=True)  23.5 us
    all_to_all x1, starting transfers between devices, local(): lax.all_to_all(lax.all_to_all(split_out, 'rep', split_axis=3, concat_axis...  14.3 us
    all_gather x1, blocking collectives, local(): full_rows = lax.all_gather(tokens, 'rep', axis=1, tiled=True)  13.1 us
    scatter x1, local copies, waits for them, and re-layouts, local(): outgoing = jnp.zeros((EXPERTS * slot_cap, width), jnp.bfloat16).at[destin...  7.66 us
    dot_general x1, matrix products, local(): jnp.einsum('esf,efd->esd', hidden, lax.all_gather(w_down, 'rep', axis=2,...  6.33 us
  transfers between devices with their start and end apart: 4, of which 2 were waited for; matrix products, arithmetic and copies ran while one was open for 8% of the time, Pallas kernels for 0%

commit v1 on v0

--- a/solution.py
+++ b/solution.py
@@ -48,7 +48,9 @@
     expert_out = jnp.einsum(
         "esf,efd->esd",
         hidden,
-        lax.all_gather(w_down, "rep", axis=2, tiled=True),
+        jnp.concatenate(
+            lax.all_to_all(jnp.stack([w_down] * lax.axis_size("rep")), "rep", 0, 0), axis=2
+        ),
         preferred_element_type=jnp.float32,
     ).astype(jnp.bfloat16)
     owners = expert_out.shape[1] // slot_cap

time: 257 us -> 243 us (0.946)
  blocking collectives: 108 us -> 35 us
  waiting for transfers between devices: 82.9 us -> 125 us
  starting transfers between devices: 14.4 us -> 30.4 us
    all_to_all x0 -> x2, waiting for transfers between devices: none -> 81.4 us  [the longest x1 51.9 us: local(): lax.all_to_all(outgoing, 'exp', split_axis=0, concat_axis=1, tiled=True)]
    all_to_all x1 -> x0, blocking collectives: 71.3 us -> none  [local(): lax.all_to_all(outgoing, 'exp', split_axis=0, concat_axis=1, tiled=True)]
    all_gather x1 -> x0, waiting for transfers between devices: 38.3 us -> none  [local(): lax.all_gather(w_down, 'rep', axis=2, tiled=True)]
    all_to_all x0 -> x2, starting transfers between devices: none -> 22.2 us  [the longest x1 17.4 us: local(): lax.all_to_all(outgoing, 'exp', split_axis=0, concat_axis=1, tiled=True)]
    all_to_all x1, starting transfers between devices: 14.3 us -> 8.22 us  [local(): lax.all_to_all(lax.all_to_all(split_out, 'rep', split_axis=3, concat_axis...]
    another operation x4 -> x6, local copies, waits for them, and re-layouts: 4.02 us -> 5.89 us
  transfers between devices with their start and end apart: 4 -> 5, of which waited for: 2 -> 3; matrix products, arithmetic and copies ran while one was open for 8% -> 9% of each run, Pallas kernels for 0% -> 0%
where the time goes in v1:
time: 243 us
  waiting for transfers between devices  125 us (51%)
  blocking collectives  35 us (14%)
  starting transfers between devices  30.4 us (13%)
  local copies, waits for them, and re-layouts  25 us (10%)
  between operations  13.6 us (6%)
  matrix products  11.3 us (5%)
    all_to_all x1, waiting for transfers between devices, local(): lax.all_to_all(outgoing, 'exp', split_axis=0, concat_axis=1, tiled=True)  51.9 us
    all_to_all x1, waiting for transfers between devices, local(): lax.all_to_all(lax.all_to_all(split_out, 'rep', split_axis=3, concat_axis...  42.4 us
    all_to_all x1, waiting for transfers between devices, local(): lax.all_to_all(jnp.stack([w_down] * lax.axis_size('rep')), 'rep', 0, 0)  29.6 us
    all_to_all x1, blocking collectives, local(): lax.all_to_all(split_out, 'rep', split_axis=3, concat_axis=3, tiled=True)  21.9 us
    all_to_all x1, starting transfers between devices, local(): lax.all_to_all(outgoing, 'exp', split_axis=0, concat_axis=1, tiled=True)  17.4 us
    all_gather x1, blocking collectives, local(): full_rows = lax.all_gather(tokens, 'rep', axis=1, tiled=True)  13.1 us
    all_to_all x1, starting transfers between devices, local(): lax.all_to_all(lax.all_to_all(split_out, 'rep', split_axis=3, concat_axis...  8.22 us
    scatter x1, local copies, waits for them, and re-layouts, local(): outgoing = jnp.zeros((EXPERTS * slot_cap, width), jnp.bfloat16).at[destin...  6.81 us
  transfers between devices with their start and end apart: 5, of which 3 were waited for; matrix products, arithmetic and copies ran while one was open for 9% of the time, Pallas kernels for 0%

profile of v1, /device:TPU:8, one launch (start us, length us, event | category | flops | bytes accessed | tf_op | source)
XLA Modules:
  0.0 242.6 jit_solution(17213516565181834792)
XLA Ops:
  6.5 0.7 all-gather.3.cloned.1.call-update
  7.3 0.9 copy.27
  9.3 0.4 fusion.19
  9.6 13.1 %all_gather.9 = bf16[128,2048]{1,0:T(8,128)(2,1)S(1)} all-gather(bf16[128,512]{1,0:T(8,128)(2,1)S(1)} %copy-done.1), channel_id=1, replica_groups=mesh['rep'=4,'exp'=128] {'rep'}, dimensions={1}, use_global_device_ids=true | all-gather | bytes 655360 | tf_op jit(solution)/shard_map/all_gather | solution.py:25
  22.8 6.8 %scatter_custom_fusion = bf16[384,2048]{1,0:T(8,128)(2,1)S(1)} fusion(s32[1024]{0:T(1024)S(1)} %bitcast.45, bf16[128,2048]{1,0:T(8,128)(2,1)S(1)} %all_gather.9, bf16[]{:T(256)} %constant.41.clone.1), kind=kCustom, calls=%fused_computation.2 | custom fusion | bytes 2097154 | tf_op jit(solution)/shard_map/scatter | solution.py:31
  29.6 2.4 reshape.201
  32.0 17.4 %all-to-all-start = ((bf16[128,3,2048]{2,1,0:T(4,128)(2,1)}), bf16[128,3,2048]{2,1,0:T(4,128)(2,1)S(1)}, u32[]{:S(2)}, u32[]{:S(2)}) async-start(bf16[128,3,2048]{2,1,0:T(4,128)(2,1)} %reshape.201), calls=%async_computation | async-start | bytes 4194304 | tf_op jit(solution)/shard_map/all_to_all | solution.py:34
  49.4 0.7 all-gather.5.cloned.1.call-update
  50.1 1.4 copy.32
  51.5 51.9 %all-to-all-done = bf16[128,3,2048]{2,1,0:T(4,128)(2,1)S(1)} async-done(((bf16[128,3,2048]{2,1,0:T(4,128)(2,1)}), bf16[128,3,2048]{2,1,0:T(4,128)(2,1)S(1)}, u32[]{:S(2)}, u32[]{:S(2)}) %all-to-all-start) | async-done | bytes 1572896 | tf_op jit(solution)/shard_map/all_to_all | solution.py:34
  103.4 1.8 stack.2
  105.2 4.8 %all-to-all-start.1 = ((bf16[4,1,768,512]{2,3,1,0:T(8,128)(2,1)}), bf16[4,1,768,512]{2,3,1,0:T(8,128)(2,1)}, u32[]{:S(2)}, u32[]{:S(2)}) async-start(bf16[4,1,768,512]{2,3,1,0:T(8,128)(2,1)} %stack.2), calls=%async_computation.1 | async-start | bytes 6291456 | tf_op jit(solution)/shard_map/all_to_all | solution.py:52
  110.0 2.5 %reshape.202 = bf16[384,2048]{1,0:T(8,128)(2,1)} reshape(bf16[128,3,2048]{2,1,0:T(4,128)(2,1)S(1)} %all-to-all-done) | data formatting | bytes 3145728 | tf_op jit(solution)/shard_map/reshape.5
  112.6 4.9 %fusion.4 = f32[384,768]{1,0:T(8,128)} fusion(bf16[384,2048]{1,0:T(8,128)(2,1)} %reshape.202, bf16[1,768,2048]{2,1,0:T(8,128)(2,1)} %all-gather.3.cloned.1.call-done), kind=kOutput, calls=%fused_computation.6 | convolution fusion | flops 1207959552 | bytes 5898240 | tf_op jit(solution)/shard_map/esd,efd->esf/dot_general | solution.py:35
  117.5 29.6 %all-to-all-done.1 = bf16[4,1,768,512]{2,3,1,0:T(8,128)(2,1)} async-done(((bf16[4,1,768,512]{2,3,1,0:T(8,128)(2,1)}), bf16[4,1,768,512]{2,3,1,0:T(8,128)(2,1)}, u32[]{:S(2)}, u32[]{:S(2)}) %all-to-all-start.1) | async-done | bytes 3145760 | tf_op jit(solution)/shard_map/all_to_all | solution.py:52
  147.1 6.3 %convolution_convert_fusion = bf16[384,2048]{1,0:T(8,128)(2,1)S(1)} fusion(bf16[768,2048]{0,1:T(8,128)(2,1)} %bitcast.11, bf16[384,2048]{1,0:T(8,128)(2,1)S(1)} %copy-done, bf16[1,768,2048]{2,1,0:T(8,128)(2,1)} %all-gather.5.cloned.1.call-done, f32[384,768]{1,0:T(8,128)} %fusion.4), kind=kOutput, calls=%fused_computation.8 | convolution fusion | flops 2418475008 | bytes 10616832 | tf_op jit(solution)/shard_map/esf,efd->esd/dot_general | solution.py:48
  153.4 1.2 reshape.207
  154.9 21.9 %all_to_all.24 = bf16[1,128,3,4,512]{4,1,2,0,3:T(8,128)(2,1)S(1)} all-to-all(bf16[1,128,3,4,512]{4,1,2,0,3:T(8,128)(2,1)S(1)} %copy.34), channel_id=1, replica_groups=mesh['rep'=4,'exp'=128] {'rep'}, dimensions={3} | all-to-all | bytes 3145728 | tf_op jit(solution)/shard_map/all_to_all | solution.py:60
  176.8 2.4 copy.35
  179.2 8.2 %all-to-all-start.3 = ((bf16[1,128,3,4,512]{4,3,2,0,1:T(4,128)(2,1)}), bf16[1,128,3,4,512]{4,3,2,0,1:T(4,128)(2,1)S(1)}, u32[]{:S(2)}, u32[]{:S(2)}) async-start(bf16[1,128,3,4,512]{4,3,2,0,1:T(4,128)(2,1)} %copy.35), calls=%async_computation.3 | async-start | bytes 3145728 | tf_op jit(solution)/shard_map/all_to_all | solution.py:59
  187.6 42.4 %all-to-all-done.3 = bf16[1,128,3,4,512]{4,3,2,0,1:T(4,128)(2,1)S(1)} async-done(((bf16[1,128,3,4,512]{4,3,2,0,1:T(4,128)(2,1)}), bf16[1,128,3,4,512]{4,3,2,0,1:T(4,128)(2,1)S(1)}, u32[]{:S(2)}, u32[]{:S(2)}) %all-to-all-start.3) | async-done | bytes 1572896 | tf_op jit(solution)/shard_map/all_to_all | solution.py:59
  230.0 0.4 reshape_transpose.3
  230.4 4.0 %gather_fusion = bf16[1024,512]{1,0:T(8,128)(2,1)S(1)} fusion(bf16[1536,512]{1,0:T(8,128)(2,1)S(1)} %reshape_transpose.3, s32[1024]{0:T(1024)S(1)} %broadcast_clamp_fusion), kind=kCustom, calls=%fused_computation | custom fusion | bytes 2101248 | tf_op jit(solution)/shard_map/gather | solution.py:67
  234.4 1.3 fusion.6
  (32 shorter events, 1.6 us)
Async XLA Ops:
  6.5 106.0 %all-gather.3.cloned.1.call-start = ((), (), s32[]{:S(2)}) async-start(), calls=%async_computation.4 | async-start | bytes 3932160 | tf_op jit(solution)/shard_map/all_gather | solution.py:38
  7.3 1.6 copy-start.2
  8.6 1.0 copy-start.1
  32.0 71.4 %all-to-all-start = ((bf16[128,3,2048]{2,1,0:T(4,128)(2,1)}), bf16[128,3,2048]{2,1,0:T(4,128)(2,1)S(1)}, u32[]{:S(2)}, u32[]{:S(2)}) async-start(bf16[128,3,2048]{2,1,0:T(4,128)(2,1)} %reshape.201), calls=%async_computation | async-start | bytes 4194304 | tf_op jit(solution)/shard_map/all_to_all | solution.py:34
  49.4 97.7 %all-gather.5.cloned.1.call-start = ((), (), s32[]{:S(2)}) async-start(), calls=%async_computation.5 | async-start | bytes 3932160 | tf_op jit(solution)/shard_map/all_gather | solution.py:44
  105.2 41.9 %all-to-all-start.1 = ((bf16[4,1,768,512]{2,3,1,0:T(8,128)(2,1)}), bf16[4,1,768,512]{2,3,1,0:T(8,128)(2,1)}, u32[]{:S(2)}, u32[]{:S(2)}) async-start(bf16[4,1,768,512]{2,3,1,0:T(8,128)(2,1)} %stack.2), calls=%async_computation.1 | async-start | bytes 6291456 | tf_op jit(solution)/shard_map/all_to_all | solution.py:52
  112.6 34.5 %copy-start = (bf16[384,2048]{1,0:T(8,128)(2,1)S(1)}, bf16[384,2048]{1,0:T(8,128)(2,1)}, u32[]{:S(2)}) copy-start(bf16[384,2048]{1,0:T(8,128)(2,1)} %reshape.202) | copy-start | bytes 4718596
  179.2 8.2 %copy-start.3 = (f32[128,8]{0,1:T(8,128)S(1)}, f32[128,8]{0,1:T(8,128)}, u32[]{:S(2)}) copy-start(f32[128,8]{0,1:T(8,128)} %param.8) | copy-start | bytes 12292
  179.2 50.8 %all-to-all-start.3 = ((bf16[1,128,3,4,512]{4,3,2,0,1:T(4,128)(2,1)}), bf16[1,128,3,4,512]{4,3,2,0,1:T(4,128)(2,1)S(1)}, u32[]{:S(2)}, u32[]{:S(2)}) async-start(bf16[1,128,3,4,512]{4,3,2,0,1:T(4,128)(2,1)} %copy.35), calls=%async_computation.3 | async-start | bytes 3145728 | tf_op jit(solution)/shard_map/all_to_all | solution.py:59
Sparse Core Ops, SparseCore 0:
  9.4 49.3 all-gather.2
  60.9 45.0 all-gather.4
